TPU v7x, 32 devices: a whole 2x2x4 slice. The times are simulated.
32 devices in a mesh: groups: 2 (over y), emit: 4 (over z), recv: 4 (over x, core).
Axes of the slice: x: 2, y: 2, z: 4, core: 2. Of those that a mesh axis runs over, the one named last changes fastest.
Arguments:
- positions: float32 [3, 8192], P(None, ('groups', 'emit', 'recv')), parts along dimension 1, may hold values from 0 to 1
- angles: float32 [2, 8192], P(None, ('groups', 'emit', 'recv')), parts along dimension 1, may hold values from -3.140625 to 3.140625
- areas: float32 [8192], P(('groups', 'emit', 'recv')), parts along dimension 0, may hold values from 0.00024414062 to 0.00390625
- emissivity: float32 [8192], P(('groups', 'emit', 'recv')), parts along dimension 0, may hold values from 0.1 to 0.9
- emission: float32 [32, 8192], P(None, ('groups', 'emit', 'recv')), parts along dimension 1, may hold values from 0.5 to 2
- radiosity_in: float32 [32, 8192], P(None, ('groups', 'emit', 'recv')), parts along dimension 1, may hold values from 0.2 to 2
- adjoint_in: float32 [32, 8192], P(None, ('groups', 'emit', 'recv')), parts along dimension 1, may hold values from 0 to 1.5
- visibility: int32 [64, 32], P(('groups', 'emit')), parts along dimension 0, may hold values 0 or 1
- inlet_patches: int32 [4096], P('groups'), parts along dimension 0, may hold values from 0 to 4095
- inlet_weights: float32 [32, 4096], P(None, 'groups'), parts along dimension 1, may hold values from 0.5 to 2
Outputs:
- radiosity_out: float32 [32, 8192], P(None, ('groups', 'emit', 'recv')), parts along dimension 1
- adjoint_out: float32 [32, 8192], P(None, ('groups', 'emit', 'recv')), parts along dimension 1
- emissivity_grad: float32 [8192], P(('groups', 'emit', 'recv')), parts along dimension 0
There are 2 independent parts, one for each index of `groups`. A program takes and returns all parts, laid end to end along the dimension named above; each array names one. Nothing has to cross between parts.
Inputs may be any that keep to these rules, and one draw needn't show every extreme that they name: `inlet_patches`: an inlet patch may be listed more than once.
All inputs are finite; a program needn't handle non-finite values. No bound on the sum of `visibility` on one device may be relied on, other than what follows from the above.
Results may differ from a plain program's by a relative error of at most 0.0003.
Values may be sent and summed in bfloat16 or wider, within the bound.
No kernel may reach another device: no remote copies, remote signals or barrier semaphores. Data moves between devices by JAX's collectives and lax.ppermute only.
A program may use at most 64 MiB of HBM per device.

v0:
```python
import math
import jax
import jax.numpy as jnp
from jax import lax
from jax.sharding import PartitionSpec as P

BLK = 128


def patch_geometry(positions, angles, areas):
    polar = angles[0]
    azimuth = angles[1]
    normal = jnp.stack(
        [jnp.sin(polar) * jnp.cos(azimuth), jnp.sin(polar) * jnp.sin(azimuth), jnp.cos(polar)]
    )
    return jnp.concatenate([positions, normal, areas[None, :]], axis=0)


def view_tile(row_geom, col_geom, block_mask):
    delta_x = col_geom[0][None, :] - row_geom[0][:, None]
    delta_y = col_geom[1][None, :] - row_geom[1][:, None]
    delta_z = col_geom[2][None, :] - row_geom[2][:, None]
    dist_sq = delta_x * delta_x + delta_y * delta_y + delta_z * delta_z
    cos_emit = jnp.maximum(
        row_geom[3][:, None] * delta_x
        + row_geom[4][:, None] * delta_y
        + row_geom[5][:, None] * delta_z,
        0.0,
    )
    cos_recv = jnp.maximum(
        -(
            col_geom[3][None, :] * delta_x
            + col_geom[4][None, :] * delta_y
            + col_geom[5][None, :] * delta_z
        ),
        0.0,
    )
    patch_area = row_geom[6][:, None]
    spread = dist_sq + patch_area
    kernel = cos_emit * cos_recv * patch_area / (math.pi * spread * spread)
    row_blocks, col_blocks = block_mask.shape
    rows_total = row_geom.shape[1]
    cols_total = col_geom.shape[1]
    expanded = jnp.broadcast_to(
        block_mask[:, None, :, None],
        (row_blocks, rows_total // row_blocks, col_blocks, cols_total // col_blocks),
    ).reshape(rows_total, cols_total)
    return (expanded * kernel).astype(jnp.bfloat16)


def block_width():
    return 128


def local(
    positions,
    angles,
    areas,
    emissivity,
    emission,
    radiosity_in,
    adjoint_in,
    visibility,
    inlet_patches,
    inlet_weights,
):
    emit_count = lax.axis_size("emit")
    recv_count = lax.axis_size("recv")
    emit_index = lax.axis_index("emit")
    recv_index = lax.axis_index("recv")
    own_count = areas.shape[0]
    cases = emission.shape[0]
    geometry = patch_geometry(positions, angles, areas)
    reflect = 1.0 - emissivity
    own_weights = (reflect[None, :] * adjoint_in).astype(jnp.bfloat16)
    own_values = radiosity_in.astype(jnp.bfloat16)
    mask_rows = visibility.shape[0]
    per_block = visibility.shape[1] // emit_count
    own_blocks = own_count // BLK
    folded_mask = visibility.astype(jnp.float32).reshape(mask_rows, emit_count, per_block)
    tile_mask = lax.dynamic_slice_in_dim(
        folded_mask, recv_index * own_blocks, own_blocks, 2
    ).reshape(mask_rows, emit_count * own_blocks)
    row_total = own_count * recv_count
    col_total = own_count * emit_count
    row_values = lax.all_gather(own_values, "recv", axis=1, tiled=True)
    col_weight = lax.all_gather(own_weights, "emit", axis=1, tiled=True)
    start_state = (
        jnp.zeros((cases, col_total), jnp.float32),
        jnp.zeros((cases, row_total), jnp.float32),
    )
    col_geom = lax.all_gather(geometry, "emit", axis=1, tiled=True)
    geom_piece = lax.all_gather(geometry, "recv", axis=1, tiled=True)
    count = geom_piece.shape[1]
    width = block_width()

    def inner(number, state):
        fwd_total, adj_total = state
        offset = number * width
        geom_part = lax.dynamic_slice_in_dim(geom_piece, offset, width, 1)
        value_part = lax.dynamic_slice_in_dim(row_values, offset, width, 1)
        mask_part = lax.dynamic_slice_in_dim(tile_mask, offset // BLK, width // BLK, 0)
        tile = view_tile(geom_part, col_geom, mask_part)
        fwd_total = fwd_total + jnp.dot(value_part, tile, preferred_element_type=jnp.float32)
        adj_part = lax.dot_general(
            col_weight, tile, (((1,), (1,)), ((), ())), preferred_element_type=jnp.float32
        )
        adj_total = lax.dynamic_update_slice_in_dim(adj_total, adj_part, offset, 1)
        return (fwd_total, adj_total)

    forward, adjoint = lax.fori_loop(0, count // width, inner, start_state)
    incoming = lax.psum_scatter(forward, "emit", scatter_dimension=1, tiled=True)
    returned = lax.psum_scatter(adjoint, "recv", scatter_dimension=1, tiled=True)
    own_ids = (emit_index * recv_count + recv_index) * own_count + lax.iota(jnp.int32, own_count)
    selector = (inlet_patches[:, None] == own_ids[None, :]).astype(jnp.float32)
    source = jnp.dot(
        inlet_weights, selector, precision=lax.Precision.HIGHEST, preferred_element_type=jnp.float32
    )
    radiosity_out = emissivity[None, :] * emission + reflect[None, :] * incoming
    adjoint_out = source + returned
    emissivity_grad = jnp.sum(adjoint_out * (emission - incoming), axis=0)
    return (radiosity_out, adjoint_out, emissivity_grad)


def solution(mesh):
    placed = (
        P(None, ("groups", "emit", "recv")),
        P(None, ("groups", "emit", "recv")),
        P(("groups", "emit", "recv")),
        P(("groups", "emit", "recv")),
        P(None, ("groups", "emit", "recv")),
        P(None, ("groups", "emit", "recv")),
        P(None, ("groups", "emit", "recv")),
        P(("groups", "emit"), None),
        P("groups"),
        P(None, "groups"),
    )
    return jax.shard_map(
        local,
        mesh=mesh,
        in_specs=placed,
        out_specs=(
            P(None, ("groups", "emit", "recv")),
            P(None, ("groups", "emit", "recv")),
            P(("groups", "emit", "recv")),
        ),
        check_vma=False,
    )
```

profile of v0, /device:TPU:0, one launch (start us, length us, event | category | flops | bytes accessed | tf_op | source)
XLA Modules:
  0.0 115.8 jit_solution(4974398801967030085)
XLA Ops:
  7.2 0.8 slice_cosine_fusion
  8.1 0.7 concatenate.3
  8.8 14.8 %all_gather.14 = f32[7,1024]{1,0:T(8,128)S(1)} all-gather(f32[7,256]{1,0:T(8,128)S(1)} %concatenate.3), channel_id=1, replica_groups=mesh['groups'=2,'emit'=4,'recv'=4] {'emit'}, dimensions={1}, use_global_device_ids=true | all-gather | bytes 35840 | tf_op jit(solution)/shard_map/all_gather | solution.py:92
  23.6 5.2 %all_gather.13 = f32[7,1024]{1,0:T(8,128)S(1)} all-gather(f32[7,256]{1,0:T(8,128)S(1)} %concatenate.3), channel_id=1, replica_groups=mesh['groups'=2,'emit'=4,'recv'=4] {'recv'}, dimensions={1}, use_global_device_ids=true | all-gather | bytes 35840 | tf_op jit(solution)/shard_map/all_gather | solution.py:93
  28.8 0.7 broadcast_subtract_fusion
  29.5 0.7 convert_element_type.21
  30.1 0.1 copy.15
  30.3 0.8 convert_element_type.20
  31.1 5.2 %all_gather.12 = bf16[32,1024]{1,0:T(8,128)(2,1)S(1)} all-gather(bf16[32,256]{1,0:T(8,128)(2,1)S(1)} %convert_element_type.20), channel_id=1, replica_groups=mesh['groups'=2,'emit'=4,'recv'=4] {'recv'}, dimensions={1}, use_global_device_ids=true | all-gather | bytes 81920 | tf_op jit(solution)/shard_map/all_gather | solution.py:86
  36.3 13.1 %all_gather.15 = bf16[32,1024]{1,0:T(8,128)(2,1)S(1)} all-gather(bf16[32,256]{1,0:T(8,128)(2,1)S(1)} %multiply_convert_fusion), channel_id=1, replica_groups=mesh['groups'=2,'emit'=4,'recv'=4] {'emit'}, dimensions={1}, use_global_device_ids=true | all-gather | bytes 81920 | tf_op jit(solution)/shard_map/all_gather | solution.py:87
  49.4 13.7 %while.18 = (s32[]{:T(128)}, f32[32,1024]{1,0:T(8,128)S(1)}, f32[32,1024]{1,0:T(8,128)S(1)}, bf16[32,1024]{1,0:T(8,128)(2,1)S(1)}, f32[8,8]{1,0:T(8,128)S(1)}, /...) while((s32[]{:T(128)}, f32[32,1024]{1,0:T(8,128)S(1)}, ...), condition=%wide.region_1.2_spmd.clone, body=%wide.region_0.1_spmd.clone.sunk | while | flops 24444952 | bytes 484852 | solution.py:111
  49.6 0.8 convolution_add_fusion.2
  50.4 0.8 fusion.47
  51.3 0.8 convolution_add_fusion.2
  52.1 0.8 fusion.47
  53.0 0.8 convolution_add_fusion.2
  53.8 0.8 fusion.47
  54.7 0.8 convolution_add_fusion.2
  55.5 0.8 fusion.47
  56.4 0.8 convolution_add_fusion.2
  57.2 0.8 fusion.47
  58.1 0.8 convolution_add_fusion.2
  58.9 0.8 fusion.47
  59.8 0.8 convolution_add_fusion.2
  60.6 0.8 fusion.47
  61.5 0.8 convolution_add_fusion.2
  62.4 0.8 fusion.47
  63.2 0.6 copy-done.1
  63.9 0.7 reduce-scatter.3.cloned.1.call-update
  64.6 20.0 %reduce-scatter.5.cloned.1.call-done = f32[32,256]{1,0:T(8,128)} async-done(((f32[32,1024]{1,0:T(8,128)}), f32[32,256]{1,0:T(8,128)}) %reduce-scatter.5.cloned.1.call-update) | async-done | bytes 32784 | tf_op jit(solution)/shard_map/reduce_scatter | solution.py:113
  84.6 21.6 %reduce-scatter.3.cloned.1.call-done = f32[32,256]{1,0:T(8,128)} async-done(((f32[32,1024]{1,0:T(8,128)}), f32[32,256]{1,0:T(8,128)}) %reduce-scatter.3.cloned.1.call-update) | async-done | bytes 32784 | tf_op jit(solution)/shard_map/reduce_scatter | solution.py:112
  106.2 2.8 %multiply_reduce_fusion = (f32[256]{0:T(256)}, f32[32,256]{1,0:T(8,128)}, f32[32,256]{1,0:T(8,128)}) fusion(f32[32,256]{1,0:T(8,128)S(1)} %copy-done.5, f32[32,256]{1,0:T(8,128)} %reduce-scatter.3.cloned.1.call-done, f32[256]{0:T(256)S(1)} %broadcast_subtract_fusion, f32[256]{0:T(256)S(1)} %copy-done.4, f32[32,256]{1,0:T(8,128)} %reduce-scatter.5.cloned.1.call-done, ...), kind=kOutput, calls=%fused_computation.47 | convolution fusion | flops 201907968 | bytes 438272 | tf_op jit(solution)/shard_map/dot_general | solution.py:116
  (62 shorter events, 1.1 us)
Async XLA Ops:
  7.2 99.0 %copy-start = (f32[32,2048]{1,0:T(8,128)S(1)}, f32[32,2048]{1,0:T(8,128)}, u32[]{:S(2)}) copy-start(f32[32,2048]{1,0:T(8,128)} %param.21) | copy-start | bytes 786436
  7.2 29.1 %copy-start.3 = (f32[32,256]{1,0:T(8,128)S(1)}, f32[32,256]{1,0:T(8,128)}, u32[]{:S(2)}) copy-start(f32[32,256]{1,0:T(8,128)} %param.18) | copy-start | bytes 98308
  7.2 77.4 %reduce-scatter.5.cloned.1.call-start = ((), (), s32[]{:S(2)}) async-start(), calls=%async_computation.3 | async-start | bytes 163840 | tf_op jit(solution)/shard_map/reduce_scatter | solution.py:113
  63.1 0.7 copy-start.1
  63.1 0.7 copy-start.2
  63.1 43.0 %copy-start.4 = (f32[256]{0:T(256)S(1)}, f32[256]{0:T(256)}, u32[]{:S(2)}) copy-start(f32[256]{0:T(256)} %param.15) | copy-start | bytes 3076
  63.2 43.0 %copy-start.5 = (f32[32,256]{1,0:T(8,128)S(1)}, f32[32,256]{1,0:T(8,128)}, u32[]{:S(2)}) copy-start(f32[32,256]{1,0:T(8,128)} %param.16) | copy-start | bytes 98308
  63.2 43.0 %copy-start.6 = (s32[2048]{0:T(1024)S(1)}, s32[2048]{0:T(1024)}, u32[]{:S(2)}) copy-start(s32[2048]{0:T(1024)} %param.20) | copy-start | bytes 24580
  63.8 42.3 %reduce-scatter.3.cloned.1.call-start = ((), (), s32[]{:S(2)}) async-start(), calls=%async_computation.2 | async-start | bytes 163840 | tf_op jit(solution)/shard_map/reduce_scatter | solution.py:112
Sparse Core Ops, SparseCore 0:
  63.9 20.5 reduce-scatter.4
  86.9 19.1 reduce-scatter.2
where the time goes:
time: 116 us
  waiting for transfers between devices  42.3 us (36%)
  blocking collectives  38.3 us (33%)
  matrix products  15.3 us (13%)
  between operations  14.1 us (12%)
  other arithmetic  2.97 us (3%)
  local copies, waits for them, and re-layouts  2.42 us (2%)
    reduce_scatter x1, waiting for transfers between devices, local(): lax.psum_scatter(forward, 'emit', scatter_dimension=1, tiled=True)  21.6 us
    reduce_scatter x1, waiting for transfers between devices, local(): lax.psum_scatter(adjoint, 'recv', scatter_dimension=1, tiled=True)  20 us
    all_gather x1, blocking collectives, local(): col_geom = lax.all_gather(geometry, 'emit', axis=1, tiled=True)  14.8 us
    all_gather x1, blocking collectives, local(): col_weight = lax.all_gather(own_weights, 'emit', axis=1, tiled=True)  13.1 us
    dot_general x8, matrix products, inner(): jnp.dot(value_part, tile, preferred_element_type=jnp.float32)  6.43 us
    dot_general x8, matrix products, inner(): lax.dot_general(col_weight, tile, (((1,), (1,)), ((), ())), preferred_ele...  6.15 us
    all_gather x1, blocking collectives, local(): row_values = lax.all_gather(own_values, 'recv', axis=1, tiled=True)  5.23 us
    all_gather x1, blocking collectives, local(): geom_piece = lax.all_gather(geometry, 'recv', axis=1, tiled=True)  5.18 us
  transfers between devices with their start and end apart: 2, of which 2 were waited for; matrix products, arithmetic and copies ran while one was open for 0% of the time, Pallas kernels for 0%

commit v1 on v0

--- a/solution.py
+++ b/solution.py
@@ -84,7 +84,15 @@
     row_total = own_count * recv_count
     col_total = own_count * emit_count
     row_values = lax.all_gather(own_values, "recv", axis=1, tiled=True)
-    col_weight = lax.all_gather(own_weights, "emit", axis=1, tiled=True)
+    x = own_weights
+    ways, here, step = (lax.axis_size("emit"), lax.axis_index("emit"), x.shape[1])
+    dims = [n * ways if d == 1 else n for d, n in enumerate(x.shape)]
+    col_weight = lax.dynamic_update_slice_in_dim(jnp.zeros(dims, x.dtype), x, here * step, axis=1)
+    for far in range(1, ways):
+        x = lax.ppermute(x, "emit", [(d, (d + 1) % ways) for d in range(ways)])
+        col_weight = lax.dynamic_update_slice_in_dim(
+            col_weight, x, (here - far) % ways * step, axis=1
+        )
     start_state = (
         jnp.zeros((cases, col_total), jnp.float32),
         jnp.zeros((cases, row_total), jnp.float32),

time: 116 us -> 109 us (0.940)
  blocking collectives: 38.3 us -> 23.8 us
  waiting for transfers between devices: 42.3 us -> 48 us
  starting transfers between devices: 0.08 us -> 3.12 us
  matrix products: 15.3 us -> 13.4 us
  other arithmetic: 2.97 us -> 4.22 us
    all_gather x1 -> x0, blocking collectives: 13.1 us -> none  [local(): col_weight = lax.all_gather(own_weights, 'emit', axis=1, tiled=True)]
    ppermute x0 -> x3, waiting for transfers between devices: none -> 11.1 us  [local(): x = lax.ppermute(x, 'emit', [(d, (d + 1) % ways) for d in range(ways)])]
    reduce_scatter x1, waiting for transfers between devices: 21.6 us -> 15.9 us  [local(): lax.psum_scatter(forward, 'emit', scatter_dimension=1, tiled=True)]
    ppermute x0 -> x3, starting transfers between devices: none -> 3.04 us  [local(): x = lax.ppermute(x, 'emit', [(d, (d + 1) % ways) for d in range(ways)])]
    reduce_sum x0 -> x1, other arithmetic: none -> 1.97 us  [local(): emissivity_grad = jnp.sum(adjoint_out * (emission - incoming), axis=0)]
    dot_general x1, matrix products: 2.76 us -> 0.8 us  [local(): jnp.dot(inlet_weights, selector, precision=lax.Precision.HIGHEST, preferr...]
    all_gather x1, blocking collectives: 14.8 us -> 13.3 us  [local(): col_geom = lax.all_gather(geometry, 'emit', axis=1, tiled=True)]
  transfers between devices with their start and end apart: 2 -> 5, of which waited for: 2 -> 4; matrix products, arithmetic and copies ran while one was open for 0% -> 2% of each run, Pallas kernels for 0% -> 0%
where the time goes in v1:
time: 109 us
  waiting for transfers between devices  48 us (44%)
  blocking collectives  23.8 us (22%)
  between operations  14.2 us (13%)
  matrix products  13.4 us (12%)
  other arithmetic  4.22 us (4%)
  starting transfers between devices  3.12 us (3%)
  local copies, waits for them, and re-layouts  1.73 us (2%)
    reduce_scatter x1, waiting for transfers between devices, local(): lax.psum_scatter(adjoint, 'recv', scatter_dimension=1, tiled=True)  20.3 us
    reduce_scatter x1, waiting for transfers between devices, local(): lax.psum_scatter(forward, 'emit', scatter_dimension=1, tiled=True)  15.9 us
    all_gather x1, blocking collectives, local(): col_geom = lax.all_gather(geometry, 'emit', axis=1, tiled=True)  13.3 us
    ppermute x3, waiting for transfers between devices, local(): x = lax.ppermute(x, 'emit', [(d, (d + 1) % ways) for d in range(ways)])  11.1 us
    dot_general x8, matrix products, inner(): jnp.dot(value_part, tile, preferred_element_type=jnp.float32)  6.43 us
    dot_general x8, matrix products, inner(): lax.dot_general(col_weight, tile, (((1,), (1,)), ((), ())), preferred_ele...  6.12 us
    all_gather x1, blocking collectives, local(): row_values = lax.all_gather(own_values, 'recv', axis=1, tiled=True)  5.25 us
    all_gather x1, blocking collectives, local(): geom_piece = lax.all_gather(geometry, 'recv', axis=1, tiled=True)  5.19 us
  transfers between devices with their start and end apart: 5, of which 4 were waited for; matrix products, arithmetic and copies ran while one was open for 2% of the time, Pallas kernels for 0%

profile of v1, /device:TPU:0, one launch (start us, length us, event | category | flops | bytes accessed | tf_op | source)
XLA Modules:
  0.0 109.0 jit_solution(10122373222317811540)
XLA Ops:
  7.3 0.7 broadcast_subtract_fusion
  8.0 0.8 constant_dynamic-update-slice_fusion.3
  8.8 3.0 %collective-permute-start = (bf16[32,256]{1,0:T(8,128)(2,1)S(1)}, bf16[32,256]{1,0:T(8,128)(2,1)S(1)}, u32[]{:S(2)}, u32[]{:S(2)}) collective-permute-start(bf16[32,256]{1,0:T(8,128)(2,1)S(1)} %get-tuple-element.259), channel_id=1, source_target_pairs={{0,4},{4,8},{8,12},{12,0},{1,5},{5,9},{9,13},{13,1},{2,6},{6,10},{... | collective-permute-start | bytes 49160 | tf_op jit(solution)/shard_map/ppermute | solution.py:92
  11.8 0.7 convert_element_type.21
  12.7 5.2 %all_gather.9 = bf16[32,1024]{1,0:T(8,128)(2,1)S(1)} all-gather(bf16[32,256]{1,0:T(8,128)(2,1)S(1)} %convert_element_type.20), channel_id=1, replica_groups=mesh['groups'=2,'emit'=4,'recv'=4] {'recv'}, dimensions={1}, use_global_device_ids=true | all-gather | bytes 81920 | tf_op jit(solution)/shard_map/all_gather | solution.py:86
  18.0 5.2 %all_gather.10 = f32[7,1024]{1,0:T(8,128)S(1)} all-gather(f32[7,256]{1,0:T(8,128)S(1)} %concatenate.3), channel_id=1, replica_groups=mesh['groups'=2,'emit'=4,'recv'=4] {'recv'}, dimensions={1}, use_global_device_ids=true | all-gather | bytes 35840 | tf_op jit(solution)/shard_map/all_gather | solution.py:101
  23.2 13.3 %all_gather.11 = f32[7,1024]{1,0:T(8,128)S(1)} all-gather(f32[7,256]{1,0:T(8,128)S(1)} %concatenate.3), channel_id=1, replica_groups=mesh['groups'=2,'emit'=4,'recv'=4] {'emit'}, dimensions={1}, use_global_device_ids=true | all-gather | bytes 35840 | tf_op jit(solution)/shard_map/all_gather | solution.py:100
  36.6 5.5 %collective-permute-done.1 = bf16[32,256]{1,0:T(8,128)(2,1)S(1)} collective-permute-done((bf16[32,256]{1,0:T(8,128)(2,1)S(1)}, bf16[32,256]{1,0:T(8,128)(2,1)S(1)}, u32[]{:S(2)}, u32[]{:S(2)}) %collective-permute-start.1) | collective-permute-done | bytes 16416 | tf_op jit(solution)/shard_map/ppermute | solution.py:92
  42.1 5.5 %collective-permute-done.2 = bf16[32,256]{1,0:T(8,128)(2,1)S(1)} collective-permute-done((bf16[32,256]{1,0:T(8,128)(2,1)S(1)}, bf16[32,256]{1,0:T(8,128)(2,1)S(1)}, u32[]{:S(2)}, u32[]{:S(2)}) %collective-permute-start.2) | collective-permute-done | bytes 16416 | tf_op jit(solution)/shard_map/ppermute | solution.py:92
  47.6 13.9 %while.18 = (s32[]{:T(128)}, f32[32,1024]{1,0:T(8,128)S(1)}, f32[32,1024]{1,0:T(8,128)S(1)}, bf16[32,1024]{1,0:T(8,128)(2,1)S(1)}, f32[8,8]{1,0:T(8,128)S(1)}, /...) while((s32[]{:T(128)}, f32[32,1024]{1,0:T(8,128)S(1)}, ...), condition=%wide.region_1.2_spmd.clone, body=%wide.region_0.1_spmd.clone.sunk | while | flops 24444952 | bytes 484844 | solution.py:119
  47.8 0.8 fusion.44
  48.6 0.8 convolution_add_fusion.2
  49.5 0.8 fusion.44
  50.3 0.8 convolution_add_fusion.2
  51.3 0.8 fusion.44
  52.0 0.8 convolution_add_fusion.2
  53.0 0.8 fusion.44
  53.8 0.8 convolution_add_fusion.2
  54.8 0.8 fusion.44
  55.5 0.8 convolution_add_fusion.2
  56.5 0.8 fusion.44
  57.3 0.8 convolution_add_fusion.2
  58.2 0.8 fusion.44
  59.0 0.8 convolution_add_fusion.2
  60.0 0.8 fusion.44
  60.7 0.8 convolution_add_fusion.2
  61.6 0.6 copy-done.2
  62.3 0.7 reduce-scatter.5.cloned.1.call-update
  63.1 0.8 fusion.23
  63.9 15.9 %reduce-scatter.3.cloned.1.call-done = f32[32,256]{1,0:T(8,128)} async-done(((f32[32,1024]{1,0:T(8,128)}), f32[32,256]{1,0:T(8,128)}) %reduce-scatter.3.cloned.1.call-update) | async-done | bytes 32784 | tf_op jit(solution)/shard_map/reduce_scatter | solution.py:120
  79.8 20.3 %reduce-scatter.5.cloned.1.call-done = f32[32,256]{1,0:T(8,128)} async-done(((f32[32,1024]{1,0:T(8,128)}), f32[32,256]{1,0:T(8,128)}) %reduce-scatter.5.cloned.1.call-update) | async-done | bytes 32784 | tf_op jit(solution)/shard_map/reduce_scatter | solution.py:121
  100.1 2.0 %multiply_reduce_fusion = (f32[256]{0:T(256)}, f32[32,256]{1,0:T(8,128)}, f32[32,256]{1,0:T(8,128)}) fusion(f32[32,256]{1,0:T(8,128)S(1)} %copy-done.3, f32[32,256]{1,0:T(8,128)} %reduce-scatter.3.cloned.1.call-done, f32[32,256]{1,0:T(8,128)S(1)} %fusion.23, f32[32,256]{1,0:T(8,128)} %reduce-scatter.5.cloned.1.call-done, f32[256]{0:T(256)S(1)} %broadcast_subtract_fusion, ...), kind=kLoop, calls=%fused_computation.46 | loop fusion | flops 57088 | bytes 199680 | tf_op jit(solution)/shard_map/reduce_sum | solution.py:129
  (78 shorter events, 1.3 us)
Async XLA Ops:
  7.2 55.8 %copy-start = (f32[32,2048]{1,0:T(8,128)S(1)}, f32[32,2048]{1,0:T(8,128)}, u32[]{:S(2)}) copy-start(f32[32,2048]{1,0:T(8,128)} %param.21) | copy-start | bytes 786436
  7.2 5.5 %copy-start.7 = (f32[2,256]{1,0:T(2,128)S(1)}, f32[2,256]{1,0:T(2,128)}, u32[]{:S(2)}) copy-start(f32[2,256]{1,0:T(2,128)} %param.13) | copy-start | bytes 6148
  7.2 5.5 %copy-start.4 = (f32[32,256]{1,0:T(8,128)S(1)}, f32[32,256]{1,0:T(8,128)}, u32[]{:S(2)}) copy-start(f32[32,256]{1,0:T(8,128)} %param.17) | copy-start | bytes 98308
  7.2 10.8 %copy-start.8 = (f32[256]{0:T(256)S(1)}, f32[256]{0:T(256)}, u32[]{:S(2)}) copy-start(f32[256]{0:T(256)} %param.14) | copy-start | bytes 3076
  7.2 10.8 %copy-start.6 = (f32[3,256]{1,0:T(4,128)S(1)}, f32[3,256]{1,0:T(4,128)}, u32[]{:S(2)}) copy-start(f32[3,256]{1,0:T(4,128)} %param.12) | copy-start | bytes 9220
  7.2 72.6 %reduce-scatter.3.cloned.1.call-start = ((), (), s32[]{:S(2)}) async-start(), calls=%async_computation.2 | async-start | bytes 163840 | tf_op jit(solution)/shard_map/reduce_scatter | solution.py:120
  8.8 27.8 %collective-permute-start = (bf16[32,256]{1,0:T(8,128)(2,1)S(1)}, bf16[32,256]{1,0:T(8,128)(2,1)S(1)}, u32[]{:S(2)}, u32[]{:S(2)}) collective-permute-start(bf16[32,256]{1,0:T(8,128)(2,1)S(1)} %get-tuple-element.259), channel_id=1, source_target_pairs={{0,4},{4,8},{8,12},{12,0},{1,5},{5,9},{9,13},{13,1},{2,6},{6,10},{... | collective-permute-start | bytes 49160 | tf_op jit(solution)/shard_map/ppermute | solution.py:92
  36.6 5.5 %collective-permute-start.1 = (bf16[32,256]{1,0:T(8,128)(2,1)S(1)}, bf16[32,256]{1,0:T(8,128)(2,1)S(1)}, u32[]{:S(2)}, u32[]{:S(2)}) collective-permute-start(bf16[32,256]{1,0:T(8,128)(2,1)S(1)} %collective-permute-done), channel_id=1, source_target_pairs={{0,4},{4,8},{8,12},{12,0},{1,5},{5,9},{9,13},{13,1},{2,6},{6,10},{... | collective-permute-start | bytes 49160 | tf_op jit(solution)/shard_map/ppermute | solution.py:92
  42.1 5.5 %collective-permute-start.2 = (bf16[32,256]{1,0:T(8,128)(2,1)S(1)}, bf16[32,256]{1,0:T(8,128)(2,1)S(1)}, u32[]{:S(2)}, u32[]{:S(2)}) collective-permute-start(bf16[32,256]{1,0:T(8,128)(2,1)S(1)} %collective-permute-done.1), channel_id=1, source_target_pairs={{0,4},{4,8},{8,12},{12,0},{1,5},{5,9},{9,13},{13,1},{2,6},{6,10},{... | collective-permute-start | bytes 49160 | tf_op jit(solution)/shard_map/ppermute | solution.py:92
  61.6 0.7 copy-start.2
  61.6 0.7 copy-start.1
  61.6 1.4 %copy-start.9 = (s32[2048]{0:T(1024)S(1)}, s32[2048]{0:T(1024)}, u32[]{:S(2)}) copy-start(s32[2048]{0:T(1024)} %param.20) | copy-start | bytes 24580
  62.2 37.9 %reduce-scatter.5.cloned.1.call-start = ((), (), s32[]{:S(2)}) async-start(), calls=%async_computation.3 | async-start | bytes 163840 | tf_op jit(solution)/shard_map/reduce_scatter | solution.py:121
  63.0 37.1 %copy-start.3 = (f32[32,256]{1,0:T(8,128)S(1)}, f32[32,256]{1,0:T(8,128)}, u32[]{:S(2)}) copy-start(f32[32,256]{1,0:T(8,128)} %param.16) | copy-start | bytes 98308
  63.0 37.1 %copy-start.5 = (f32[256]{0:T(256)S(1)}, f32[256]{0:T(256)}, u32[]{:S(2)}) copy-start(f32[256]{0:T(256)} %param.15) | copy-start | bytes 3076
Sparse Core Ops, SparseCore 0:
  62.4 17.3 reduce-scatter.2
  82.4 17.7 reduce-scatter.4
